TPU v7x, 32 devices: a whole 2x2x4 slice. The times are simulated.
32 devices in a mesh: member: 2 (over y), lat: 16 (over z, x, core).
Axes of the slice: x: 2, y: 2, z: 4, core: 2. Of those that a mesh axis runs over, the one named last changes fastest.
Arguments:
- increment: float32 [274, 256, 128], P('member', 'lat'), parts along dimension 0, may hold values from -6 to 6
- filter_taps: int32 [4, 2, 2, 5], replicated, may hold values from 1 to 8
- band_roots: float32 [5, 137, 137], replicated, may hold values from -1 to 1
Outputs:
- adjoint: float32 [274, 256, 128], P('member', 'lat'), parts along dimension 0
There are 2 independent parts, one for each index of `member`. A program takes and returns all parts, laid end to end along the dimension named above; an argument that names none is the same for every part. Nothing has to cross between parts.
All inputs are finite; a program needn't handle non-finite values.
Results may differ from a plain program's by a relative error of at most 0.0001.
Values sent between devices are 32-bit elements; how exact they have to be, the bound alone decides.
A program may use at most 64 MiB of HBM per device.

v0:
```python
import functools
import math

import jax
import jax.numpy as jnp
from jax import lax
from jax.experimental import pallas as pl
from jax.experimental.pallas import tpu as pltpu
from jax.sharding import PartitionSpec as P

LEVELS = 4
ROOT_TWO = math.sqrt(2.0)
F32, BF16 = jnp.float32, jnp.bfloat16


def make_filters(filter_taps):
    coeffs = filter_taps.astype(F32)
    signs = jnp.array([1.0, -1.0, 1.0, -1.0, 1.0], dtype=F32)
    lowpass = ROOT_TWO * coeffs[:, :, 0] / jnp.sum(coeffs[:, :, 0], axis=-1, keepdims=True)
    highpass = (
        signs
        * coeffs[:, :, 1]
        / jnp.sqrt(jnp.sum(coeffs[:, :, 1] * coeffs[:, :, 1], axis=-1, keepdims=True))
    )
    return jnp.stack([lowpass, highpass], axis=2)


def halves_of(x):
    high = x.astype(BF16)
    return high, (x - high.astype(F32)).astype(BF16)


def dot(a, b):
    return jnp.dot(a, b, preferred_element_type=F32)


def kernel(lats, taps, x_hbm, roots, out, *scratch):
    xs = (scratch[0:4], (scratch[4],) + scratch[5:8])
    tops, hs, lvs = scratch[8], scratch[9:13], scratch[13:17]
    gs = (scratch[17:21], scratch[21:25])
    ks = (scratch[25:29], scratch[29:33])
    wmats, mats, sends, recvs, load_sem = scratch[33:]
    tile, lev, lanes = x_hbm.shape
    me = lax.axis_index("lat")
    has_down, has_up = me > 0, me < lats - 1
    slots = iter(range(10_000))

    def tap(level, direction, kind, k):
        return taps[((level * 2 + direction) * 2 + kind) * 5 + k]

    def exchange(src_up, dst_up, src_down, dst_down):
        up_slot, down_slot = next(slots), next(slots)
        up = pltpu.make_async_remote_copy(
            src_ref=src_up, dst_ref=dst_up, send_sem=sends.at[up_slot],
            recv_sem=recvs.at[up_slot], device_id={"lat": jnp.minimum(me + 1, lats - 1)},
            device_id_type=pl.DeviceIdType.MESH,
        )
        down = pltpu.make_async_remote_copy(
            src_ref=src_down, dst_ref=dst_down, send_sem=sends.at[down_slot],
            recv_sem=recvs.at[down_slot], device_id={"lat": jnp.maximum(me - 1, 0)},
            device_id_type=pl.DeviceIdType.MESH,
        )

        @pl.when(has_up)
        def _():
            up.start()

        @pl.when(has_down)
        def _():
            down.start()

        def arrive():
            @pl.when(has_down)
            def _():
                up.wait_recv()

            @pl.when(has_up)
            def _():
                down.wait_recv()

        def sent():
            @pl.when(has_up)
            def _():
                up.wait_send()

            @pl.when(has_down)
            def _():
                down.wait_send()

        pending.append(sent)
        return arrive

    pending = []
    load = pltpu.make_async_copy(x_hbm, xs[0][0].at[pl.ds(2, tile)], load_sem)
    load.start()

    barrier = pltpu.get_barrier_semaphore()

    @pl.when(has_down)
    def _():
        pl.semaphore_signal(
            barrier, inc=1, device_id={"lat": jnp.maximum(me - 1, 0)},
            device_id_type=pl.DeviceIdType.MESH,
        )

    @pl.when(has_up)
    def _():
        pl.semaphore_signal(
            barrier, inc=1, device_id={"lat": jnp.minimum(me + 1, lats - 1)},
            device_id_type=pl.DeviceIdType.MESH,
        )

    pl.semaphore_wait(barrier, has_down.astype(jnp.int32) + has_up.astype(jnp.int32))

    arrive = exchange(
        x_hbm.at[pl.ds(tile - 2, 2)], xs[0][0].at[pl.ds(0, 2)],
        x_hbm.at[pl.ds(0, 1)], xs[0][0].at[pl.ds(tile + 2, 1)],
    )

    def zeros(ref, start, count):
        for r in range(count):
            ref[start + r] = jnp.zeros(ref.shape[1:], F32)

    rims = []
    for t in range(2):
        for j in range(LEVELS):
            n = tile >> (j + 1)
            if not (t == 1 and j == 0):
                rims.append((xs[t][j], 2, 1, 2 * n + 2))
            rim = 2 if t == 0 and j == 0 else 1
            rims.append((gs[t][j], rim, rim, n + rim))
            rims.append((ks[t][j], rim, rim, n + rim))

    @pl.when(jnp.logical_not(has_down))
    def _():
        for ref, below, _, _ in rims:
            zeros(ref, 0, below)

    @pl.when(jnp.logical_not(has_up))
    def _():
        for ref, _, above, at in rims:
            zeros(ref, at, above)

    for j in range(LEVELS):
        width = lanes >> j
        for flip in range(2):
            c = lax.broadcasted_iota(jnp.int32, (lanes, lanes), flip)
            o = lax.broadcasted_iota(jnp.int32, (lanes, lanes), 1 - flip)
            is_low = o < width // 2
            t = c - 2 * jnp.where(is_low, o, o - width // 2) + 2
            w = jnp.zeros((lanes, lanes), F32)
            for k in range(5):
                w = jnp.where(t == k, jnp.where(is_low, tap(j, 1, 0, k), tap(j, 1, 1, k)), w)
            w = jnp.where((c < width) & (o < width), w, 0.0)
            high, low = halves_of(w)
            at = 2 * j + flip
            wmats[at, pl.ds(0, lanes), pl.ds(0, lanes)] = high
            wmats[at, pl.ds(0, lanes), pl.ds(lanes, lanes)] = low
            wmats[at, pl.ds(lanes, lanes), pl.ds(0, lanes)] = high
            wmats[at, pl.ds(lanes, lanes), pl.ds(lanes, lanes)] = jnp.zeros_like(low)
    for b in range(roots.shape[0]):
        high, low = halves_of(roots[b])
        mats[b, pl.ds(0, lev)] = high
        mats[b, pl.ds(lev, lev)] = low

    def along_lon(x, at):
        high, low = halves_of(x)
        r = dot(jnp.concatenate([high, low], axis=1), wmats[at])
        return r[:, :lanes] + r[:, lanes:]

    def vertical(x, t, band):
        b = t * (LEVELS + 1) + band
        high, low = halves_of(x)
        r = dot(mats[b], high)
        return r[:lev] + r[lev:] + dot(mats[b, pl.ds(0, lev)], low)

    def loop(start, stop, body):
        if stop - start == 1:
            body(start)
        elif stop > start:
            lax.fori_loop(start, stop, lambda i, _: (body(i), 0)[1], 0)

    lane = lax.broadcasted_iota(jnp.int32, (lev, lanes), 1)

    def transform(t, arrive):
        k_arrivals = [None] * LEVELS
        for j in range(LEVELS):
            n = tile >> (j + 1)
            x = xs[t][j]
            following = xs[t][j + 1] if j + 1 < LEVELS else tops
            lead = 2 if j + 1 < LEVELS else 0

            def analyse(i):
                rows = [x[2 * i + k] for k in range(5)]
                low = sum(tap(j, 0, 0, k) * rows[k] for k in range(5))
                high = sum(tap(j, 0, 1, k) * rows[k] for k in range(5))
                both = along_lon(jnp.concatenate([low, high], axis=0), 2 * j)
                following[i + lead] = both[:lev]
                hs[j][i] = both[lev:]

            loop(1, n - 1, analyse)
            if arrive is not None:
                arrive()
            analyse(0)
            if n > 1:
                analyse(n - 1)
            arrive = None
            if j + 1 < LEVELS:
                arrive = exchange(
                    following.at[pl.ds(n, 2)], following.at[pl.ds(0, 2)],
                    following.at[pl.ds(2, 1)], following.at[pl.ds(n + 2, 1)],
                )
            rim = 2 if t == 0 and j == 0 else 1
            k_ref = ks[t][j]

            def weigh(i):
                pair = jnp.concatenate([following[i + lead], hs[j][i]], axis=1)
                pair = vertical(pair, t, j)
                lvs[j][i] = pair[:, :lanes]
                k_ref[i + rim] = along_lon(pair[:, lanes:], 2 * j + 1)

            loop(0, n, weigh)
            k_arrivals[j] = exchange(
                k_ref.at[pl.ds(n, rim)], k_ref.at[pl.ds(0, rim)],
                k_ref.at[pl.ds(rim, rim)], k_ref.at[pl.ds(n + rim, rim)],
            )
        for j in reversed(range(LEVELS)):
            n = tile >> (j + 1)
            rim = 2 if t == 0 and j == 0 else 1
            g_ref, k_ref = gs[t][j], ks[t][j]

            def lift(i, coarse):
                chosen = jnp.where(lane < (lanes >> (j + 1)), coarse, lvs[j][i])
                g_ref[i + rim] = along_lon(chosen, 2 * j + 1)

            if j == LEVELS - 1:
                lift(0, vertical(tops[0], t, LEVELS))
            else:
                def both(m, lift=lift, make=make):
                    even, odd = make(m)
                    lift(2 * m, even)
                    lift(2 * m + 1, odd)

                loop(0, n // 2, both)
            g_arrive = exchange(
                g_ref.at[pl.ds(n, rim)], g_ref.at[pl.ds(0, rim)],
                g_ref.at[pl.ds(rim, rim)], g_ref.at[pl.ds(n + rim, rim)],
            )
            k_arrivals[j]()
            g_arrive()

            def make(m, j=j, rim=rim, g_ref=g_ref, k_ref=k_ref, even_only=False):
                g = [g_ref[m + rim + s] for s in ((-1, 0, 1))]
                k = [k_ref[m + rim + s] for s in ((-1, 0, 1))]
                even = sum(tap(j, 0, 0, 4 - 2 * s) * g[s] + tap(j, 0, 1, 4 - 2 * s) * k[s] for s in range(3))
                if even_only:
                    return even
                odd = (
                    tap(j, 0, 0, 3) * g[1] + tap(j, 0, 0, 1) * g[2]
                    + tap(j, 0, 1, 3) * k[1] + tap(j, 0, 1, 1) * k[2]
                )
                return even, odd

        return make

    load.wait()
    make = transform(0, arrive)
    shaped = xs[1][0]

    def keep(m):
        shaped[2 * m + 2], shaped[2 * m + 3] = make(m)

    loop(0, tile // 2, keep)
    even, odd = make(-1)
    inside = jnp.where(has_down, 1.0, 0.0).astype(F32)
    shaped[0], shaped[1] = inside * even, inside * odd
    shaped[tile + 2] = jnp.where(has_up, 1.0, 0.0).astype(F32) * make(tile // 2, even_only=True)

    make = transform(1, None)

    def put(m):
        out[2 * m], out[2 * m + 1] = make(m)

    loop(0, tile // 2, put)
    for sent in pending:
        sent()


def on_device(increment, filter_taps, band_roots, lats):
    lev, tile, lanes = increment.shape
    padded = -(-lev // 16) * 16
    taps = make_filters(filter_taps).reshape(-1)
    x = jnp.pad(jnp.transpose(increment, (1, 0, 2)), ((0, 0), (0, padded - lev), (0, 0)))
    roots = jnp.pad(band_roots, ((0, 0), (0, padded - lev), (0, padded - lev)))
    roots = jnp.concatenate([roots, jnp.swapaxes(roots, 1, 2)])

    def slabs(count):
        return pltpu.VMEM((count, padded, lanes), F32)

    counts = [tile >> (j + 1) for j in range(LEVELS)]
    scratch = [slabs(2 * n + 3) for n in counts] * 2
    scratch += [slabs(1)] + [slabs(n) for n in counts] * 2
    for _ in range(2):
        scratch += [slabs(n + (4 if j == 0 else 2)) for j, n in enumerate(counts)]
        scratch += [slabs(n + 2) for n in counts]
    copies = 2 * (LEVELS + 2 * LEVELS) * 2 - 2
    scratch += [
        pltpu.VMEM((2 * LEVELS, 2 * lanes, 2 * lanes), BF16),
        pltpu.VMEM((2 * (LEVELS + 1), 2 * padded, padded), BF16),
        pltpu.SemaphoreType.DMA((copies,)),
        pltpu.SemaphoreType.DMA((copies,)),
        pltpu.SemaphoreType.DMA,
    ]
    y = pl.pallas_call(
        functools.partial(kernel, lats),
        out_shape=jax.ShapeDtypeStruct((tile, padded, lanes), F32),
        in_specs=[
            pl.BlockSpec(memory_space=pltpu.SMEM),
            pl.BlockSpec(memory_space=pl.ANY),
            pl.BlockSpec(memory_space=pltpu.VMEM),
        ],
        out_specs=pl.BlockSpec(memory_space=pltpu.VMEM),
        scratch_shapes=scratch,
        compiler_params=pltpu.CompilerParams(
            collective_id=0, has_side_effects=True, vmem_limit_bytes=48 << 20
        ),
    )(taps, x, roots)
    return jnp.transpose(y[:, :lev], (1, 0, 2))


def solution(mesh):
    placed = (P("member", "lat", None), P(), P())
    return jax.shard_map(
        functools.partial(on_device, lats=mesh.shape["lat"]),
        mesh=mesh, in_specs=placed, out_specs=P("member", "lat", None), check_vma=False,
    )
```

profile of v0, /device:TPU:21, one launch (start us, length us, event | category | flops | bytes accessed | tf_op | source)
XLA Modules:
  0.0 79.7 jit_solution(4701724086028409743)
XLA Ops:
  0.0 0.7 convert_element_type.7
  0.7 0.1 slice_reduce_fusion
  0.8 0.7 multiply_divide_fusion.1
  1.6 0.1 reshape.10.taps
  1.7 1.5 %copy.6 = f32[5,137,137]{1,2,0:T(8,128)S(1)} copy(f32[5,137,137]{2,1,0:T(8,128)} %param.6) | data formatting | bytes 750760 | tf_op args[2]
  3.2 0.1 pad_bitcast_fusion
  3.3 0.4 copy.10
  3.6 0.1 pad.9.clone
  3.7 0.0 copy-start
  3.7 0.1 pad_maximum_fusion.roots
  3.8 1.1 %copy-done = f32[137,16,128]{2,1,0:T(8,128)S(1)} copy-done((f32[137,16,128]{2,1,0:T(8,128)S(1)}, f32[137,16,128]{2,1,0:T(8,128)}, u32[]{:S(2)}) %copy-start) | copy-done | bytes 1122328
  4.9 0.4 copy.11
  5.3 0.1 pad.8.x_hbm
  5.4 72.9 %shard_map.46 = f32[16,144,128]{2,1,0:T(8,128)S(1)} custom-call(f32[80]{0:T(128)S(1)} %reshape.10.taps, f32[16,144,128]{2,1,0:T(8,128)S(1)} %pad.8.x_hbm, f32[10,144,144]{2,1,0:T(8,128)S(1)} %pad_maximum_fusion.roots), custom_call_target="tpu_custom_call" | custom-call | tf_op jit(solution)/shard_map/pallas_call | solution.py:314
  78.3 0.1 slice_bitcast_fusion
  78.4 1.3 %copy.8 = f32[137,16,128]{2,1,0:T(8,128)} copy(f32[137,16,128]{2,0,1:T(8,128)S(1)} %slice_bitcast_fusion) | data formatting | bytes 2244608 | tf_op jit(solution)/shard_map/transpose | solution.py:328
  (2 shorter events, 0.0 us)
Async XLA Ops:
  3.7 1.3 %copy-start = (f32[137,16,128]{2,1,0:T(8,128)S(1)}, f32[137,16,128]{2,1,0:T(8,128)}, u32[]{:S(2)}) copy-start(f32[137,16,128]{2,1,0:T(8,128)} %param.4) | copy-start | bytes 3366916
where the time goes:
time: 79.9 us; the launch traced here: 79.7 us
  Pallas kernels  72.9 us (91%)
  local copies, waits for them, and re-layouts  5.05 us (6%)
  other arithmetic  1.68 us (2%)
    pallas_call x1, Pallas kernels, on_device(): pl.pallas_call(functools.partial(kernel, lats), out_shape=jax.ShapeDtypeS...  72.9 us
    unnamed x5, local copies, waits for them, and re-layouts  3.35 us

commit v1 on v0

v1 whole, which is shorter than its diff:
```python
import functools
import math

import jax
import jax.numpy as jnp
from jax import lax
from jax.experimental import pallas as pl
from jax.experimental.pallas import tpu as pltpu
from jax.sharding import PartitionSpec as P

LEVELS = 4
ROOT_TWO = math.sqrt(2.0)
F32, BF16 = jnp.float32, jnp.bfloat16


def make_filters(filter_taps):
    coeffs = filter_taps.astype(F32)
    signs = jnp.array([1.0, -1.0, 1.0, -1.0, 1.0], dtype=F32)
    lowpass = ROOT_TWO * coeffs[:, :, 0] / jnp.sum(coeffs[:, :, 0], axis=-1, keepdims=True)
    highpass = (
        signs
        * coeffs[:, :, 1]
        / jnp.sqrt(jnp.sum(coeffs[:, :, 1] * coeffs[:, :, 1], axis=-1, keepdims=True))
    )
    return jnp.stack([lowpass, highpass], axis=2)


def halves_of(x):
    high = x.astype(BF16)
    return high, (x - high.astype(F32)).astype(BF16)


def dot(a, b):
    return jnp.dot(a, b, preferred_element_type=F32)


def kernel(lats, taps, x_hbm, roots, out, *scratch):
    scratch = iter(scratch)

    def take(count):
        return [next(scratch) for _ in range(count)]

    xs = [take(LEVELS), take(LEVELS)]
    packs = [take(LEVELS - 1), take(LEVELS - 1)]
    lands = [take(LEVELS - 1), take(LEVELS - 1)]
    gs = [take(LEVELS), take(LEVELS)]
    ks = take(2)
    parts = take(LEVELS)
    hs, top = take(2)
    wmats, mats, sends, recvs, load_sem = scratch
    tile, lev, lanes = x_hbm.shape
    half = lanes // 2
    me = lax.axis_index("lat")
    has_down, has_up = me > 0, me < lats - 1
    above = {"lat": jnp.minimum(me + 1, lats - 1)}
    below = {"lat": jnp.maximum(me - 1, 0)}
    mesh_ids = pl.DeviceIdType.MESH
    slots = iter(range(10_000))
    pending = []

    def tap(level, direction, kind, k):
        return taps[((level * 2 + direction) * 2 + kind) * 5 + k]

    def exchange(src_up, dst_up, src_down, dst_down):
        up_slot, down_slot = next(slots), next(slots)
        up = pltpu.make_async_remote_copy(
            src_ref=src_up, dst_ref=dst_up, send_sem=sends.at[up_slot],
            recv_sem=recvs.at[up_slot], device_id=above, device_id_type=mesh_ids,
        )
        down = pltpu.make_async_remote_copy(
            src_ref=src_down, dst_ref=dst_down, send_sem=sends.at[down_slot],
            recv_sem=recvs.at[down_slot], device_id=below, device_id_type=mesh_ids,
        )

        @pl.when(has_up)
        def _():
            up.start()

        @pl.when(has_down)
        def _():
            down.start()

        def arrive():
            @pl.when(has_down)
            def _():
                up.wait_recv()

            @pl.when(has_up)
            def _():
                down.wait_recv()

        def sent():
            @pl.when(has_up)
            def _():
                up.wait_send()

            @pl.when(has_down)
            def _():
                down.wait_send()

        pending.append(sent)
        return arrive

    load = pltpu.make_async_copy(x_hbm, xs[0][0].at[pl.ds(2, tile)], load_sem)
    load.start()

    barrier = pltpu.get_barrier_semaphore()

    @pl.when(has_down)
    def _():
        pl.semaphore_signal(barrier, inc=1, device_id=below, device_id_type=mesh_ids)

    @pl.when(has_up)
    def _():
        pl.semaphore_signal(barrier, inc=1, device_id=above, device_id_type=mesh_ids)

    pl.semaphore_wait(barrier, has_down.astype(jnp.int32) + has_up.astype(jnp.int32))

    arrive = exchange(
        x_hbm.at[pl.ds(tile - 2, 2)], xs[0][0].at[pl.ds(0, 2)],
        x_hbm.at[pl.ds(0, 1)], xs[0][0].at[pl.ds(tile + 2, 1)],
    )

    def clear(ref, start, count):
        for r in range(count):
            ref[start + r] = jnp.zeros(ref.shape[1:], F32)

    edges_low, edges_high = [(xs[0][0], 0, 2)], [(xs[0][0], tile + 2, 1)]
    for t in range(2):
        for j in range(LEVELS):
            n = tile >> (j + 1)
            if j:
                edges_low.append((lands[t][j - 1], 0, 1))
                edges_high.append((xs[t][j], 2 * n + 2, 1))
            rim = 2 if t == 0 and j == 0 else 1
            edges_low.append((gs[t][j], 0, rim))
            edges_high.append((gs[t][j], n + rim, rim))
        rim = 2 - t
        edges_low.append((ks[t], 0, rim))
        edges_high.append((ks[t], tile // 2 + rim, rim))

    @pl.when(jnp.logical_not(has_down))
    def _():
        for edge in edges_low:
            clear(*edge)

    @pl.when(jnp.logical_not(has_up))
    def _():
        for edge in edges_high:
            clear(*edge)

    for j in range(LEVELS):
        width = lanes >> j
        block = lanes if j == 0 else half
        for flip in range(2):
            c = lax.broadcasted_iota(jnp.int32, (lanes, lanes), flip)
            o = lax.broadcasted_iota(jnp.int32, (lanes, lanes), 1 - flip)
            same = True
            if j:
                same = (c < half) == (o < half)
                c = jnp.where(c < half, c, c - half)
                o = jnp.where(o < half, o, o - half)
            is_low = o < width // 2
            t = c - 2 * jnp.where(is_low, o, o - width // 2) + 2
            w = jnp.zeros((lanes, lanes), F32)
            for k in range(5):
                w = jnp.where(t == k, jnp.where(is_low, tap(j, 1, 0, k), tap(j, 1, 1, k)), w)
            w = jnp.where((c < width) & (o < width) & same, w, 0.0)
            high, low = halves_of(w)
            at = 2 * j + flip
            wmats[at, pl.ds(0, lanes), pl.ds(0, lanes)] = high
            wmats[at, pl.ds(0, lanes), pl.ds(lanes, lanes)] = low
            wmats[at, pl.ds(lanes, lanes), pl.ds(0, lanes)] = high
            wmats[at, pl.ds(lanes, lanes), pl.ds(lanes, lanes)] = jnp.zeros_like(low)
    for b in range(roots.shape[0]):
        high, low = halves_of(roots[b])
        mats[b, pl.ds(0, lev)] = high
        mats[b, pl.ds(lev, lev)] = low

    def along_lon(x, at):
        high, low = halves_of(x)
        r = dot(jnp.concatenate([high, low], axis=1), wmats[at])
        return r[:, :lanes] + r[:, lanes:]

    def vertical(x, t, band):
        b = t * (LEVELS + 1) + band
        high, low = halves_of(x)
        r = dot(mats[b], high)
        return r[:lev] + r[lev:] + dot(mats[b, pl.ds(0, lev)], low)

    def loop(start, stop, body, step=2):
        count = max(stop - start, 0)
        whole = count // step
        if whole > 1:
            def several(i, _):
                for s in range(step):
                    body(start + i * step + s)
                return 0

            lax.fori_loop(0, whole, several, 0)
        else:
            whole = 0
        for i in range(start + whole * step, stop):
            body(i)

    lane = lax.broadcasted_iota(jnp.int32, (lev, lanes), 1)
    lane8 = lax.broadcasted_iota(jnp.int32, (8, lanes), 1)

    def swap(x):
        return pltpu.roll(x, half, 1)

    def twice(x):
        return jnp.where(lane < half, x, swap(x))

    def weighted(level, pairs):
        total = None
        for k, x in pairs:
            scale = jnp.where(lane8 < half, tap(level, 0, 0, k), tap(level, 0, 1, k))
            term = scale[None] * x.reshape(lev // 8, 8, lanes)
            total = term if total is None else total + term
        return total.reshape(lev, lanes)

    def analyse_first(t, i):
        rows = [xs[t][0][2 * i + k] for k in range(5)]
        low = sum(tap(0, 0, 0, k) * rows[k] for k in range(5))
        high = sum(tap(0, 0, 1, k) * rows[k] for k in range(5))
        both = along_lon(jnp.concatenate([low, high], axis=0), 0)
        parts[0][i] = both[:lev]
        hs[i] = both[lev:]
        xs[t][1][i + 2] = twice(both[:lev])

    def analyse(t, j, i):
        x = xs[t][j]
        part = along_lon(weighted(j, [(k, x[2 * i + k]) for k in range(5)]), 2 * j)
        parts[j][i] = part
        if j + 1 < LEVELS:
            xs[t][j + 1][i + 2] = twice(part)
        else:
            top[0] = part

    def share_coarse(t, j):
        rows, pack, land = xs[t][j], packs[t][j - 1], lands[t][j - 1]
        count = tile >> j
        pack[0] = jnp.where(lane < half, rows[count], rows[count + 1])
        wait = exchange(pack, land, rows.at[pl.ds(2, 1)], rows.at[pl.ds(count + 2, 1)])

        def arrived():
            wait()
            got = land[0]
            turned = swap(got)
            rows[0] = jnp.where(lane < half, got, turned)
            rows[1] = jnp.where(lane < half, turned, got)

        return arrived

    def share(ref, n, rim):
        return exchange(
            ref.at[pl.ds(n, rim)], ref.at[pl.ds(0, rim)],
            ref.at[pl.ds(rim, rim)], ref.at[pl.ds(n + rim, rim)],
        )

    def weigh_first(t, i):
        pair = vertical(jnp.concatenate([parts[0][i], hs[i]], axis=1), t, 0)
        parts[0][i] = pair[:, :lanes]
        ks[t][i + 2 - t] = along_lon(pair[:, lanes:], 1)

    def weigh(t, j):
        n = tile >> (j + 1)
        for i in range(0, n, 2):
            count = min(2, n - i)
            pair = [parts[j][i + s] for s in range(count)]
            pair = vertical(jnp.concatenate(pair, axis=1), t, j)
            for s in range(count):
                parts[j][i + s] = pair[:, s * lanes:(s + 1) * lanes]

    def lift(t, j, i, coarse):
        chosen = jnp.where(lane < (lanes >> (j + 1)), coarse, parts[j][i])
        rim = 2 if t == 0 and j == 0 else 1
        gs[t][j][i + rim] = along_lon(chosen, 2 * j + 1)

    def make(t, j, m):
        g = [gs[t][j][m + s] for s in range(3)]
        even = weighted(j, [(4 - 2 * s, g[s]) for s in range(3)])
        odd = weighted(j, [(5 - 2 * s, g[s]) for s in (1, 2)])
        return even + swap(even), odd + swap(odd)

    def make_first(t, m, even_only=False):
        rim = 2 - t
        g = [gs[t][0][m + rim + s] for s in (-1, 0, 1)]
        k = [ks[t][m + rim + s] for s in (-1, 0, 1)]
        even = sum(tap(0, 0, 0, 4 - 2 * s) * g[s] + tap(0, 0, 1, 4 - 2 * s) * k[s] for s in range(3))
        if even_only:
            return even
        odd = sum(tap(0, 0, 0, 5 - 2 * s) * g[s] + tap(0, 0, 1, 5 - 2 * s) * k[s] for s in (1, 2))
        return even, odd

    def middle(t):
        first_n = tile // 2
        arrived = share_coarse(t, 1)
        loop(0, first_n, lambda i: weigh_first(t, i))
        k_arrive = None
        for j in range(1, LEVELS):
            n = tile >> (j + 1)
            loop(1, n - 1, lambda i: analyse(t, j, i))
            arrived()
            analyse(t, j, 0)
            if n > 1:
                analyse(t, j, n - 1)
            if j + 1 < LEVELS:
                arrived = share_coarse(t, j + 1)
            if k_arrive is None:
                k_arrive = share(ks[t], first_n, 2 - t)
            if j + 1 < LEVELS:
                weigh(t, j)
        weigh(t, LEVELS - 1)
        lift(t, LEVELS - 1, 0, vertical(top[0], t, LEVELS))
        for j in reversed(range(1, LEVELS)):
            n = tile >> (j + 1)
            g_arrive = share(gs[t][j], n, 1)

            def both(m):
                even, odd = make(t, j, m)
                lift(t, j - 1, 2 * m, even)
                lift(t, j - 1, 2 * m + 1, odd)

            loop(1, n - 1, both, 1)
            g_arrive()
            both(0)
            if n > 1:
                both(n - 1)
        g_arrive = share(gs[t][0], first_n, 2 - t)

        def arrive_all():
            k_arrive()
            g_arrive()

        return arrive_all

    n = tile // 2
    load.wait()
    loop(1, n - 1, lambda i: analyse_first(0, i))
    arrive()
    analyse_first(0, 0)
    analyse_first(0, n - 1)
    arrive = middle(0)
    shaped = xs[1][0]

    def keep(m):
        shaped[2 * m + 2], shaped[2 * m + 3] = make_first(0, m)

    loop(1, n - 1, keep)
    loop(2, n - 2, lambda i: analyse_first(1, i))
    arrive()
    keep(0)
    keep(n - 1)
    even, odd = make_first(0, -1)
    inside = jnp.where(has_down, 1.0, 0.0).astype(F32)
    shaped[0], shaped[1] = inside * even, inside * odd
    shaped[tile + 2] = jnp.where(has_up, 1.0, 0.0).astype(F32) * make_first(0, n, even_only=True)
    for i in (0, 1, n - 2, n - 1):
        analyse_first(1, i)
    arrive = middle(1)

    def put(m):
        out[2 * m], out[2 * m + 1] = make_first(1, m)

    loop(1, n - 1, put)
    arrive()
    put(0)
    put(n - 1)
    for sent in pending:
        sent()


def on_device(increment, filter_taps, band_roots, lats):
    lev, tile, lanes = increment.shape
    padded = -(-lev // 16) * 16
    taps = make_filters(filter_taps).reshape(-1)
    x = jnp.pad(jnp.transpose(increment, (1, 0, 2)), ((0, 0), (0, padded - lev), (0, 0)))
    roots = jnp.pad(band_roots, ((0, 0), (0, padded - lev), (0, padded - lev)))
    roots = jnp.concatenate([roots, jnp.swapaxes(roots, 1, 2)])

    def slabs(count):
        return pltpu.VMEM((count, padded, lanes), F32)

    counts = [tile >> (j + 1) for j in range(LEVELS)]
    scratch = [slabs(2 * n + 3) for n in counts] * 2
    scratch += [slabs(1)] * (4 * (LEVELS - 1))
    scratch += [slabs(n + (4 if j == 0 else 2)) for j, n in enumerate(counts)]
    scratch += [slabs(n + 2) for n in counts]
    scratch += [slabs(counts[0] + 4), slabs(counts[0] + 2)]
    scratch += [slabs(n) for n in counts] + [slabs(counts[0]), slabs(1)]
    copies = 2 * (2 * LEVELS + 2 * (LEVELS - 1) + 3)
    scratch += [
        pltpu.VMEM((2 * LEVELS, 2 * lanes, 2 * lanes), BF16),
        pltpu.VMEM((2 * (LEVELS + 1), 2 * padded, padded), BF16),
        pltpu.SemaphoreType.DMA((copies,)),
        pltpu.SemaphoreType.DMA((copies,)),
        pltpu.SemaphoreType.DMA,
    ]
    y = pl.pallas_call(
        functools.partial(kernel, lats),
        out_shape=jax.ShapeDtypeStruct((tile, padded, lanes), F32),
        in_specs=[
            pl.BlockSpec(memory_space=pltpu.SMEM),
            pl.BlockSpec(memory_space=pl.ANY),
            pl.BlockSpec(memory_space=pltpu.VMEM),
        ],
        out_specs=pl.BlockSpec(memory_space=pltpu.VMEM),
        scratch_shapes=scratch,
        compiler_params=pltpu.CompilerParams(
            collective_id=0, has_side_effects=True, vmem_limit_bytes=48 << 20
        ),
    )(taps, x, roots)
    return jnp.transpose(y[:, :lev], (1, 0, 2))


def solution(mesh):
    placed = (P("member", "lat", None), P(), P())
    return jax.shard_map(
        functools.partial(on_device, lats=mesh.shape["lat"]),
        mesh=mesh, in_specs=placed, out_specs=P("member", "lat", None), check_vma=False,
    )
```

time: 79.9 us -> 69.1 us (0.86)
  the two profiles are of different devices: /device:TPU:21 before, /device:TPU:9 now
where the time goes in v1:
time: 69.1 us; the launch traced here: 68.8 us
  Pallas kernels  62 us (90%)
  local copies, waits for them, and re-layouts  5.05 us (7%)
  other arithmetic  1.68 us (2%)
    pallas_call x1, Pallas kernels, on_device(): pl.pallas_call(functools.partial(kernel, lats), out_shape=jax.ShapeDtypeS...  62 us
    unnamed x5, local copies, waits for them, and re-layouts  3.35 us
    transpose x2, local copies, waits for them, and re-layouts, on_device(): return jnp.transpose(y[:, :lev], (1, 0, 2))  1.42 us

profile of v1, /device:TPU:9, one launch (start us, length us, event | category | flops | bytes accessed | tf_op | source)
XLA Modules:
  0.0 68.8 jit_solution(4389660704575019782)
XLA Ops:
  0.0 0.7 %convert_element_type.7 = f32[4,2,2,5]{3,2,1,0:T(2,128)S(1)} convert(s32[4,2,2,5]{3,2,1,0:T(2,128)} %param.5) | non-fusion elementwise | flops 80 | bytes 640 | tf_op jit(solution)/shard_map/convert_element_type | solution.py:17
  0.7 0.1 slice_reduce_fusion
  0.8 0.7 %multiply_divide_fusion.1 = (f32[4,2,1,5]{3,2,1,0:T(1,128)S(1)}, f32[4,2,1,5]{3,2,1,0:T(1,128)S(1)}) fusion(f32[4,2,2,5]{3,2,1,0:T(2,128)S(1)} %convert_element_type.7, f32[4,2]{1,0:T(4,128)S(1)} %get-tuple-element.5, f32[4,2]{1,0:T(4,128)S(1)} %sqrt.8, f32[5]{0:T(128)} %constant.8.clone), kind=kLoop, calls=%fused_computation.6 | loop fusion | flops 160 | bytes 724 | tf_op jit(solution)/shard_map/div | solution.py:19
  1.6 0.1 reshape.10.taps
  1.7 1.5 %copy.6 = f32[5,137,137]{1,2,0:T(8,128)S(1)} copy(f32[5,137,137]{2,1,0:T(8,128)} %param.6) | data formatting | bytes 750760 | tf_op args[2]
  3.2 0.1 pad_bitcast_fusion
  3.3 0.4 copy.10
  3.6 0.1 pad.9.clone
  3.7 0.0 copy-start
  3.7 0.1 pad_maximum_fusion.roots
  3.8 1.1 %copy-done = f32[137,16,128]{2,1,0:T(8,128)S(1)} copy-done((f32[137,16,128]{2,1,0:T(8,128)S(1)}, f32[137,16,128]{2,1,0:T(8,128)}, u32[]{:S(2)}) %copy-start) | copy-done | bytes 1122328
  4.9 0.4 copy.11
  5.3 0.1 pad.8.x_hbm
  5.4 62.0 %shard_map.46 = f32[16,144,128]{2,1,0:T(8,128)S(1)} custom-call(f32[80]{0:T(128)S(1)} %reshape.10.taps, f32[16,144,128]{2,1,0:T(8,128)S(1)} %pad.8.x_hbm, f32[10,144,144]{2,1,0:T(8,128)S(1)} %pad_maximum_fusion.roots), custom_call_target="tpu_custom_call" | custom-call | tf_op jit(solution)/shard_map/pallas_call | solution.py:401
  67.4 0.1 slice_bitcast_fusion
  67.5 1.3 %copy.8 = f32[137,16,128]{2,1,0:T(8,128)} copy(f32[137,16,128]{2,0,1:T(8,128)S(1)} %slice_bitcast_fusion) | data formatting | bytes 2244608 | tf_op jit(solution)/shard_map/transpose | solution.py:415
  (2 shorter events, 0.0 us)
Async XLA Ops:
  3.7 1.3 %copy-start = (f32[137,16,128]{2,1,0:T(8,128)S(1)}, f32[137,16,128]{2,1,0:T(8,128)}, u32[]{:S(2)}) copy-start(f32[137,16,128]{2,1,0:T(8,128)} %param.4) | copy-start | bytes 3366916

commit v2 on v1

v2 whole, which is shorter than its diff:
```python
import functools
import math

import jax
import jax.numpy as jnp
from jax import lax
from jax.experimental import pallas as pl
from jax.experimental.pallas import tpu as pltpu
from jax.sharding import PartitionSpec as P

LEVELS = 4
NEAR, NEAR_T, FAR, FAR_T = 5, 8, 12, 17
REACH = (1, -1, 2, -2, 3, -3)
ROOT_TWO = math.sqrt(2.0)
F32, BF16 = jnp.float32, jnp.bfloat16


def make_filters(filter_taps):
    coeffs = filter_taps.astype(F32)
    signs = jnp.array([1.0, -1.0, 1.0, -1.0, 1.0], dtype=F32)
    lowpass = ROOT_TWO * coeffs[:, :, 0] / jnp.sum(coeffs[:, :, 0], axis=-1, keepdims=True)
    highpass = (
        signs
        * coeffs[:, :, 1]
        / jnp.sqrt(jnp.sum(coeffs[:, :, 1] * coeffs[:, :, 1], axis=-1, keepdims=True))
    )
    return jnp.stack([lowpass, highpass], axis=2)


def halves_of(x):
    high = x.astype(BF16)
    return high, (x - high.astype(F32)).astype(BF16)


def dot(a, b):
    return jnp.dot(a, b, preferred_element_type=F32)


def kernel(lats, taps, x_hbm, roots, out, *scratch):
    scratch = iter(scratch)

    def take(count):
        return [next(scratch) for _ in range(count)]

    xs = [take(2), take(2)]
    packs, lands = take(2), take(2)
    wides, seconds = take(2), take(2)
    gs, ks = take(2), take(2)
    g_second, part, hs, cats = take(4)
    wmats, mats, sends, recvs, load_sem = scratch
    tile, lev, lanes = x_hbm.shape
    half = lanes // 2
    me = lax.axis_index("lat")
    has_down, has_up = me > 0, me < lats - 1
    mesh_ids = pl.DeviceIdType.MESH
    slots = iter(range(10_000))
    pending = []

    def tap(level, direction, kind, k):
        return taps[((level * 2 + direction) * 2 + kind) * 5 + k]

    def device(d):
        return {"lat": jnp.clip(me + d, 0, lats - 1)}

    def there(d):
        return me + d < lats if d > 0 else me + d >= 0

    def exchange(moves):
        waits = []
        for d, src, dst in moves:
            slot = next(slots)
            copy = pltpu.make_async_remote_copy(
                src_ref=src, dst_ref=dst, send_sem=sends.at[slot],
                recv_sem=recvs.at[slot], device_id=device(d), device_id_type=mesh_ids,
            )
            waits.append((d, copy))
            pl.when(there(d))(copy.start)
            pending.append(lambda d=d, copy=copy: pl.when(there(d))(copy.wait_send))

        def arrive():
            for d, copy in waits:
                pl.when(there(-d))(copy.wait_recv)

        return arrive

    load = pltpu.make_async_copy(x_hbm, xs[0][0].at[pl.ds(2, tile)], load_sem)
    load.start()

    barrier = pltpu.get_barrier_semaphore()

    peers = 0
    for d in REACH:
        def greet(d=d):
            pl.semaphore_signal(barrier, inc=1, device_id=device(d), device_id_type=mesh_ids)

        pl.when(there(d))(greet)
        peers = peers + there(d).astype(jnp.int32)
    pl.semaphore_wait(barrier, peers)

    arrive = exchange([
        (1, x_hbm.at[pl.ds(tile - 2, 2)], xs[0][0].at[pl.ds(0, 2)]),
        (-1, x_hbm.at[pl.ds(0, 1)], xs[0][0].at[pl.ds(tile + 2, 1)]),
    ])

    def clear(ref, start, count):
        for r in range(count):
            ref[start + r] = jnp.zeros(ref.shape[1:], F32)

    half_rows, quarter = tile // 2, tile // 4
    edges_low, edges_high = [(xs[0][0], 0, 2)], [(xs[0][0], tile + 2, 1)]
    for t in range(2):
        rim = 2 - t
        edges_low += [(lands[t], 0, 1), (gs[t], 0, rim), (ks[t], 0, rim), (seconds[t], 0, 1)]
        edges_high += [(xs[t][1], half_rows + 2, 1), (gs[t], half_rows + rim, rim)]
        edges_high += [(ks[t], half_rows + rim, rim), (seconds[t], quarter + 1, 1)]

    @pl.when(jnp.logical_not(has_down))
    def _():
        for edge in edges_low:
            clear(*edge)

    @pl.when(jnp.logical_not(has_up))
    def _():
        for edge in edges_high:
            clear(*edge)

    for d in REACH:
        def blank(d=d):
            for t in range(2):
                clear(wides[t], 3 + d, 1)

        pl.when(jnp.logical_not(there(d)))(blank)
    cats[7] = jnp.zeros(cats.shape[1:], BF16)

    def keep_matrix(at, w):
        high, low = halves_of(w)
        wmats[at, pl.ds(0, lanes), pl.ds(0, lanes)] = high
        wmats[at, pl.ds(0, lanes), pl.ds(lanes, lanes)] = low
        wmats[at, pl.ds(lanes, lanes), pl.ds(0, lanes)] = high
        wmats[at, pl.ds(lanes, lanes), pl.ds(lanes, lanes)] = jnp.zeros_like(low)

    def build_wide(at, level, shift, flip):
        width = lanes >> level
        c = lax.broadcasted_iota(jnp.int32, (lanes, lanes), flip)
        o = lax.broadcasted_iota(jnp.int32, (lanes, lanes), 1 - flip)
        pitch = width if level == 2 else 4 * width
        row, col = c // pitch, c % pitch
        out_row, kind, out_col = o // (2 * width), (o // width) % 2, o % width
        is_low = out_col < width // 2
        t = col - 2 * jnp.where(is_low, out_col, out_col - width // 2) + 2
        u = row + shift - 2 * out_row + 2
        lon = jnp.zeros((lanes, lanes), F32)
        lat = jnp.zeros((lanes, lanes), F32)
        for k in range(5):
            lon = jnp.where(t == k, jnp.where(is_low, tap(level, 1, 0, k), tap(level, 1, 1, k)), lon)
            lat = jnp.where(u == k, jnp.where(kind == 0, tap(level, 0, 0, k), tap(level, 0, 1, k)), lat)
        keep_matrix(at, jnp.where(col < width, lon * lat, 0.0))

    def build_second():
        for q in (-1, 0, 1):
            build_wide(NEAR + q, 2, 4 * q, 0)
            build_wide(NEAR_T + q, 2, 4 * q, 1)

    def build_third():
        for q in range(-2, 4):
            build_wide(FAR + q, 3, 2 * q + 2, 0)
            if -2 < q < 2:
                build_wide(FAR_T + q, 3, 2 * q + 2, 1)

    for j in range(2):
        width = lanes >> j
        block = lanes if j == 0 else half
        for flip in range(2):
            c = lax.broadcasted_iota(jnp.int32, (lanes, lanes), flip)
            o = lax.broadcasted_iota(jnp.int32, (lanes, lanes), 1 - flip)
            same = True
            if j:
                same = (c < half) == (o < half)
                c = jnp.where(c < half, c, c - half)
                o = jnp.where(o < half, o, o - half)
            is_low = o < width // 2
            t = c - 2 * jnp.where(is_low, o, o - width // 2) + 2
            w = jnp.zeros((lanes, lanes), F32)
            for k in range(5):
                w = jnp.where(t == k, jnp.where(is_low, tap(j, 1, 0, k), tap(j, 1, 1, k)), w)
            w = jnp.where((c < width) & (o < width) & same, w, 0.0)
            keep_matrix(2 * j + flip, w)
    for b in range(roots.shape[0]):
        high, low = halves_of(roots[b])
        mats[b, pl.ds(0, lev)] = high
        mats[b, pl.ds(lev, lev)] = low

    def along_lon(x, at):
        high, low = halves_of(x)
        r = dot(jnp.concatenate([high, low], axis=1), wmats[at])
        return r[:, :lanes] + r[:, lanes:]

    def vertical(x, t, band):
        b = t * (LEVELS + 1) + band
        high, low = halves_of(x)
        r = dot(mats[b], high)
        return r[:lev] + r[lev:] + dot(mats[b, pl.ds(0, lev)], low)

    def loop(start, stop, body, step=2):
        count = max(stop - start, 0)
        whole = count // step
        if whole > 1:
            def several(i, _):
                for s in range(step):
                    body(start + i * step + s)
                return 0

            lax.fori_loop(0, whole, several, 0)
        else:
            whole = 0
        for i in range(start + whole * step, stop):
            body(i)

    lane = lax.broadcasted_iota(jnp.int32, (lev, lanes), 1)
    lane8 = lax.broadcasted_iota(jnp.int32, (8, lanes), 1)

    def swap(x):
        return pltpu.roll(x, half, 1)

    def twice(x):
        return jnp.where(lane < half, x, swap(x))

    def weighted(level, pairs):
        total = None
        for k, x in pairs:
            scale = jnp.where(lane8 < half, tap(level, 0, 0, k), tap(level, 0, 1, k))
            term = scale[None] * x.reshape(lev // 8, 8, lanes)
            total = term if total is None else total + term
        return total.reshape(lev, lanes)

    def analyse_first(t, i):
        rows = [xs[t][0][2 * i + k] for k in range(5)]
        low = sum(tap(0, 0, 0, k) * rows[k] for k in range(5))
        high = sum(tap(0, 0, 1, k) * rows[k] for k in range(5))
        both = along_lon(jnp.concatenate([low, high], axis=0), 0)
        part[i] = both[:lev]
        hs[i] = both[lev:]
        xs[t][1][i + 2] = twice(both[:lev])

    def analyse(t, i):
        rows = [(k, xs[t][1][2 * i + k]) for k in range(5)]
        seconds[t][i + 1] = along_lon(weighted(1, rows), 2)

    def share_coarse(t):
        rows, pack, land = xs[t][1], packs[t], lands[t]
        pack[0] = jnp.where(lane < half, rows[half_rows], rows[half_rows + 1])
        wait = exchange([
            (1, pack, land),
            (-1, rows.at[pl.ds(2, 1)], rows.at[pl.ds(half_rows + 2, 1)]),
        ])

        def arrived():
            wait()
            got = land[0]
            turned = swap(got)
            rows[0] = jnp.where(lane < half, got, turned)
            rows[1] = jnp.where(lane < half, turned, got)

        return arrived

    def share(ref, n, rim):
        return exchange([
            (1, ref.at[pl.ds(n, rim)], ref.at[pl.ds(0, rim)]),
            (-1, ref.at[pl.ds(rim, rim)], ref.at[pl.ds(n + rim, rim)]),
        ])

    def weigh_first(t, i):
        pair = vertical(jnp.concatenate([part[i], hs[i]], axis=1), t, 0)
        part[i] = pair[:, :lanes]
        ks[t][i + 2 - t] = along_lon(pair[:, lanes:], 1)

    def weigh_second(t):
        for i in range(0, quarter, 2):
            pair = [seconds[t][i + s + 1] for s in range(2)]
            pair = vertical(jnp.concatenate(pair, axis=1), t, 1)
            for s in range(2):
                seconds[t][i + s + 1] = pair[:, s * lanes:(s + 1) * lanes]

    def lift_second(t, i, coarse):
        chosen = jnp.where(lane < lanes // 4, coarse, seconds[t][i + 1])
        return along_lon(chosen, 3)

    def lift_first(t, i, coarse):
        chosen = jnp.where(lane < half, coarse, part[i])
        gs[t][i + 2 - t] = along_lon(chosen, 1)

    def make(m):
        g = [g_second[m + s] for s in range(3)]
        even = weighted(1, [(4 - 2 * s, g[s]) for s in range(3)])
        odd = weighted(1, [(5 - 2 * s, g[s]) for s in (1, 2)])
        return even + swap(even), odd + swap(odd)

    def make_first(t, m, even_only=False):
        rim = 2 - t
        g = [gs[t][m + rim + s] for s in (-1, 0, 1)]
        k = [ks[t][m + rim + s] for s in (-1, 0, 1)]
        even = sum(tap(0, 0, 0, 4 - 2 * s) * g[s] + tap(0, 0, 1, 4 - 2 * s) * k[s] for s in range(3))
        if even_only:
            return even
        odd = sum(tap(0, 0, 0, 5 - 2 * s) * g[s] + tap(0, 0, 1, 5 - 2 * s) * k[s] for s in (1, 2))
        return even, odd

    def joined(x):
        return jnp.concatenate(halves_of(x), axis=1)

    def folded(r):
        return r[:, :lanes] + r[:, lanes:]

    def present(s):
        return jnp.where((me + s >= 0) & (me + s < lats), 1.0, 0.0).astype(F32)

    def cat_rows(start, count):
        return cats[pl.ds(start, count)].reshape(count * lev, 2 * lanes)

    def deep(t):
        for s in range(7):
            cats[s] = joined(wides[t][s])
        q = dot(cat_rows(1, 6), wmats[NEAR])
        q = folded(q + dot(cat_rows(0, 6), wmats[NEAR - 1]) + dot(cat_rows(2, 6), wmats[NEAR + 1]))
        q = [present(s - 2) * q[s * lev:(s + 1) * lev] for s in range(6)]
        third = folded(sum(dot(joined(q[s]), wmats[FAR + s - 2]) for s in range(6)))
        owner = me + lane // (lanes // 4) - 1
        third = jnp.where((owner >= 0) & (owner < lats), third, 0.0)
        top = vertical(third, t, LEVELS)
        third = jnp.where(lane % (lanes // 4) < lanes // 16, top, vertical(third, t, 3))
        third = joined(third)
        second = vertical(jnp.concatenate(q[1:4], axis=1), t, 2)
        lifted = []
        for s in (-1, 0, 1):
            c = folded(dot(third, wmats[FAR_T + s]))
            d = second[:, (s + 1) * lanes:(s + 2) * lanes]
            lifted.append(joined(present(s) * jnp.where(lane % half < lanes // 8, c, d)))

        def spread(pairs):
            return folded(sum(dot(lifted[s + 1], wmats[NEAR_T + d]) for s, d in pairs))

        return (
            spread(((-1, 0), (0, -1))),
            spread(((-1, 1), (0, 0), (1, -1))),
            spread(((0, 1), (1, 0))),
        )

    def middle(t):
        arrived = share_coarse(t)
        if t == 0:
            build_second()
        loop(0, half_rows, lambda i: weigh_first(t, i))
        loop(1, quarter - 1, lambda i: analyse(t, i))
        arrived()
        analyse(t, 0)
        analyse(t, quarter - 1)
        own = seconds[t][1]
        for r in range(1, quarter):
            turned = pltpu.roll(seconds[t][r + 1], r * (lanes // 4), 1)
            own = jnp.where(lane < r * (lanes // 4), own, turned)
        wide = wides[t]
        wide[3] = own
        arrived = exchange([(d, wide.at[pl.ds(3, 1)], wide.at[pl.ds(3 - d, 1)]) for d in REACH])
        weigh_second(t)
        second_arrive = share(seconds[t], quarter, 1)
        k_arrive = share(ks[t], half_rows, 2 - t)
        if t == 0:
            build_third()
        arrived()
        before, own, after = deep(t)
        for r in range(quarter):
            coarse = own if r == 0 else pltpu.roll(own, lanes - r * (lanes // 4), 1)
            g_second[r + 1] = lift_second(t, r, coarse)

        def both(m):
            even, odd = make(m)
            lift_first(t, 2 * m, even)
            lift_first(t, 2 * m + 1, odd)

        second_arrive()
        before = pltpu.roll(before, lanes // 4, 1)
        g_second[0] = present(-1) * lift_second(t, -1, before)
        g_second[quarter + 1] = present(1) * lift_second(t, quarter, after)
        both(0)
        both(quarter - 1)
        g_arrive = share(gs[t], half_rows, 2 - t)
        loop(1, quarter - 1, both, 1)

        def arrive_all():
            k_arrive()
            g_arrive()

        return arrive_all

    n = tile // 2
    load.wait()
    loop(1, n - 1, lambda i: analyse_first(0, i))
    arrive()
    analyse_first(0, 0)
    analyse_first(0, n - 1)
    arrive = middle(0)
    shaped = xs[1][0]

    def keep(m):
        shaped[2 * m + 2], shaped[2 * m + 3] = make_first(0, m)

    loop(1, n - 1, keep)
    loop(2, n - 2, lambda i: analyse_first(1, i))
    arrive()
    keep(0)
    keep(n - 1)
    even, odd = make_first(0, -1)
    inside = jnp.where(has_down, 1.0, 0.0).astype(F32)
    shaped[0], shaped[1] = inside * even, inside * odd
    shaped[tile + 2] = jnp.where(has_up, 1.0, 0.0).astype(F32) * make_first(0, n, even_only=True)
    for i in (0, 1, n - 2, n - 1):
        analyse_first(1, i)
    arrive = middle(1)

    def put(m):
        out[2 * m], out[2 * m + 1] = make_first(1, m)

    loop(1, n - 1, put)
    arrive()
    put(0)
    put(n - 1)
    for sent in pending:
        sent()


def on_device(increment, filter_taps, band_roots, lats):
    lev, tile, lanes = increment.shape
    padded = -(-lev // 16) * 16
    taps = make_filters(filter_taps).reshape(-1)
    x = jnp.pad(jnp.transpose(increment, (1, 0, 2)), ((0, 0), (0, padded - lev), (0, 0)))
    roots = jnp.pad(band_roots, ((0, 0), (0, padded - lev), (0, padded - lev)))
    roots = jnp.concatenate([roots, jnp.swapaxes(roots, 1, 2)])

    def slabs(count):
        return pltpu.VMEM((count, padded, lanes), F32)

    counts = [tile >> (j + 1) for j in range(LEVELS)]
    scratch = [slabs(2 * n + 3) for n in counts[:2]] * 2
    scratch += [slabs(1)] * 4 + [slabs(7)] * 2 + [slabs(counts[1] + 2)] * 2
    scratch += [slabs(counts[0] + 4), slabs(counts[0] + 2)] * 2
    scratch += [slabs(counts[1] + 2), slabs(counts[0]), slabs(counts[0])]
    scratch += [pltpu.VMEM((8, padded, 2 * lanes), BF16)]
    copies = 2 + 2 * (2 + len(REACH) + 2 * 3)
    scratch += [
        pltpu.VMEM((FAR_T + 2, 2 * lanes, 2 * lanes), BF16),
        pltpu.VMEM((2 * (LEVELS + 1), 2 * padded, padded), BF16),
        pltpu.SemaphoreType.DMA((copies,)),
        pltpu.SemaphoreType.DMA((copies,)),
        pltpu.SemaphoreType.DMA,
    ]
    y = pl.pallas_call(
        functools.partial(kernel, lats),
        out_shape=jax.ShapeDtypeStruct((tile, padded, lanes), F32),
        in_specs=[
            pl.BlockSpec(memory_space=pltpu.SMEM),
            pl.BlockSpec(memory_space=pl.ANY),
            pl.BlockSpec(memory_space=pltpu.VMEM),
        ],
        out_specs=pl.BlockSpec(memory_space=pltpu.VMEM),
        scratch_shapes=scratch,
        compiler_params=pltpu.CompilerParams(
            collective_id=0, has_side_effects=True, vmem_limit_bytes=48 << 20
        ),
    )(taps, x, roots)
    return jnp.transpose(y[:, :lev], (1, 0, 2))


def solution(mesh):
    placed = (P("member", "lat", None), P(), P())
    return jax.shard_map(
        functools.partial(on_device, lats=mesh.shape["lat"]),
        mesh=mesh, in_specs=placed, out_specs=P("member", "lat", None), check_vma=False,
    )
```

time: 69.1 us -> 56.7 us (0.82)
  the two profiles are of different devices: /device:TPU:9 before, /device:TPU:3 now
where the time goes in v2:
time: 56.7 us; the launch traced here: 56.5 us
  Pallas kernels  49.6 us (87%)
  local copies, waits for them, and re-layouts  5.05 us (9%)
  other arithmetic  1.68 us (3%)
    pallas_call x1, Pallas kernels, on_device(): pl.pallas_call(functools.partial(kernel, lats), out_shape=jax.ShapeDtypeS...  49.6 us
    unnamed x5, local copies, waits for them, and re-layouts  3.35 us
    transpose x2, local copies, waits for them, and re-layouts, on_device(): return jnp.transpose(y[:, :lev], (1, 0, 2))  1.42 us

profile of v2, /device:TPU:3, one launch (start us, length us, event | category | flops | bytes accessed | tf_op | source)
XLA Modules:
  0.0 56.5 jit_solution(7032956270341846508)
XLA Ops:
  0.0 0.7 %convert_element_type.7 = f32[4,2,2,5]{3,2,1,0:T(2,128)S(1)} convert(s32[4,2,2,5]{3,2,1,0:T(2,128)} %param.5) | non-fusion elementwise | flops 80 | bytes 640 | tf_op jit(solution)/shard_map/convert_element_type | solution.py:19
  0.7 0.1 slice_reduce_fusion
  0.8 0.7 %multiply_divide_fusion.1 = (f32[4,2,1,5]{3,2,1,0:T(1,128)S(1)}, f32[4,2,1,5]{3,2,1,0:T(1,128)S(1)}) fusion(f32[4,2,2,5]{3,2,1,0:T(2,128)S(1)} %convert_element_type.7, f32[4,2]{1,0:T(4,128)S(1)} %get-tuple-element.5, f32[4,2]{1,0:T(4,128)S(1)} %sqrt.8, f32[5]{0:T(128)} %constant.8.clone), kind=kLoop, calls=%fused_computation.6 | loop fusion | flops 160 | bytes 724 | tf_op jit(solution)/shard_map/div | solution.py:21
  1.6 0.1 reshape.10.taps
  1.7 1.5 %copy.6 = f32[5,137,137]{1,2,0:T(8,128)S(1)} copy(f32[5,137,137]{2,1,0:T(8,128)} %param.6) | data formatting | bytes 750760 | tf_op args[2]
  3.2 0.1 pad_bitcast_fusion
  3.3 0.4 copy.10
  3.6 0.1 pad.9.clone
  3.7 0.0 copy-start
  3.7 0.1 pad_maximum_fusion.roots
  3.8 1.1 %copy-done = f32[137,16,128]{2,1,0:T(8,128)S(1)} copy-done((f32[137,16,128]{2,1,0:T(8,128)S(1)}, f32[137,16,128]{2,1,0:T(8,128)}, u32[]{:S(2)}) %copy-start) | copy-done | bytes 1122328
  4.9 0.4 copy.11
  5.3 0.1 pad.8.x_hbm
  5.4 49.6 %shard_map.46 = f32[16,144,128]{2,1,0:T(8,128)S(1)} custom-call(f32[80]{0:T(128)S(1)} %reshape.10.taps, f32[16,144,128]{2,1,0:T(8,128)S(1)} %pad.8.x_hbm, f32[10,144,144]{2,1,0:T(8,128)S(1)} %pad_maximum_fusion.roots), custom_call_target="tpu_custom_call" | custom-call | tf_op jit(solution)/shard_map/pallas_call | solution.py:456
  55.0 0.1 slice_bitcast_fusion
  55.1 1.3 %copy.8 = f32[137,16,128]{2,1,0:T(8,128)} copy(f32[137,16,128]{2,0,1:T(8,128)S(1)} %slice_bitcast_fusion) | data formatting | bytes 2244608 | tf_op jit(solution)/shard_map/transpose | solution.py:470
  (2 shorter events, 0.0 us)
Async XLA Ops:
  3.7 1.3 %copy-start = (f32[137,16,128]{2,1,0:T(8,128)S(1)}, f32[137,16,128]{2,1,0:T(8,128)}, u32[]{:S(2)}) copy-start(f32[137,16,128]{2,1,0:T(8,128)} %param.4) | copy-start | bytes 3366916

commit v3 on v2

--- a/solution.py
+++ b/solution.py
@@ -15,18 +15,6 @@
 F32, BF16 = jnp.float32, jnp.bfloat16
 
 
-def make_filters(filter_taps):
-    coeffs = filter_taps.astype(F32)
-    signs = jnp.array([1.0, -1.0, 1.0, -1.0, 1.0], dtype=F32)
-    lowpass = ROOT_TWO * coeffs[:, :, 0] / jnp.sum(coeffs[:, :, 0], axis=-1, keepdims=True)
-    highpass = (
-        signs
-        * coeffs[:, :, 1]
-        / jnp.sqrt(jnp.sum(coeffs[:, :, 1] * coeffs[:, :, 1], axis=-1, keepdims=True))
-    )
-    return jnp.stack([lowpass, highpass], axis=2)
-
-
 def halves_of(x):
     high = x.astype(BF16)
     return high, (x - high.astype(F32)).astype(BF16)
@@ -36,7 +24,7 @@
     return jnp.dot(a, b, preferred_element_type=F32)
 
 
-def kernel(lats, taps, x_hbm, roots, out, *scratch):
+def kernel(lats, raw_taps, x_hbm, roots_hbm, out, *scratch):
     scratch = iter(scratch)
 
     def take(count):
@@ -47,7 +35,7 @@
     wides, seconds = take(2), take(2)
     gs, ks = take(2), take(2)
     g_second, part, hs, cats = take(4)
-    wmats, mats, sends, recvs, load_sem = scratch
+    wmats, mats, taps, roots, square, sends, recvs, load_sem, root_sem = scratch
     tile, lev, lanes = x_hbm.shape
     half = lanes // 2
     me = lax.axis_index("lat")
@@ -85,6 +73,8 @@
 
     load = pltpu.make_async_copy(x_hbm, xs[0][0].at[pl.ds(2, tile)], load_sem)
     load.start()
+    fetch = pltpu.make_async_copy(roots_hbm, roots, root_sem)
+    fetch.start()
 
     barrier = pltpu.get_barrier_semaphore()
 
@@ -101,6 +91,16 @@
         (1, x_hbm.at[pl.ds(tile - 2, 2)], xs[0][0].at[pl.ds(0, 2)]),
         (-1, x_hbm.at[pl.ds(0, 1)], xs[0][0].at[pl.ds(tile + 2, 1)]),
     ])
+
+    for f in range(4 * LEVELS):
+        values = [raw_taps[f * 5 + k].astype(F32) for k in range(5)]
+        if f % 2:
+            total = jnp.full((8, lanes), sum(v * v for v in values), F32)
+            scale = (1.0 / jnp.sqrt(total))[0, 0]
+        else:
+            scale = (ROOT_TWO / jnp.full((8, lanes), sum(values), F32))[0, 0]
+        for k in range(5):
+            taps[f * 5 + k] = values[k] * (-scale if f % 2 and k % 2 else scale)
 
     def clear(ref, start, count):
         for r in range(count):
@@ -185,10 +185,16 @@
                 w = jnp.where(t == k, jnp.where(is_low, tap(j, 1, 0, k), tap(j, 1, 1, k)), w)
             w = jnp.where((c < width) & (o < width) & same, w, 0.0)
             keep_matrix(2 * j + flip, w)
-    for b in range(roots.shape[0]):
-        high, low = halves_of(roots[b])
-        mats[b, pl.ds(0, lev)] = high
-        mats[b, pl.ds(lev, lev)] = low
+    fetch.wait()
+    square[...] = jnp.zeros(square.shape, F32)
+    count = roots.shape[1]
+    for b in range(LEVELS + 1):
+        square[pl.ds(0, count), pl.ds(0, count)] = roots[b]
+        whole = square[...]
+        for t, m in enumerate((whole, whole.T)):
+            high, low = halves_of(m[:lev, :lev])
+            mats[t * (LEVELS + 1) + b, pl.ds(0, lev)] = high
+            mats[t * (LEVELS + 1) + b, pl.ds(lev, lev)] = low
 
     def along_lon(x, at):
         high, low = halves_of(x)
@@ -317,19 +323,29 @@
     def cat_rows(start, count):
         return cats[pl.ds(start, count)].reshape(count * lev, 2 * lanes)
 
-    def deep(t):
-        for s in range(7):
+    def deep(t, near_arrive, far_arrive):
+        def coarsen(start, count):
+            q = dot(cat_rows(start, count), wmats[NEAR])
+            q = q + dot(cat_rows(start - 1, count), wmats[NEAR - 1])
+            q = folded(q + dot(cat_rows(start + 1, count), wmats[NEAR + 1]))
+            return [present(start + s - 3) * q[s * lev:(s + 1) * lev] for s in range(count)]
+
+        near_arrive()
+        for s in range(1, 6):
             cats[s] = joined(wides[t][s])
-        q = dot(cat_rows(1, 6), wmats[NEAR])
-        q = folded(q + dot(cat_rows(0, 6), wmats[NEAR - 1]) + dot(cat_rows(2, 6), wmats[NEAR + 1]))
-        q = [present(s - 2) * q[s * lev:(s + 1) * lev] for s in range(6)]
-        third = folded(sum(dot(joined(q[s]), wmats[FAR + s - 2]) for s in range(6)))
+        middle_q = coarsen(2, 3)
+        second = vertical(jnp.concatenate(middle_q, axis=1), t, 2)
+        partial = sum(dot(joined(middle_q[s]), wmats[FAR + s - 1]) for s in range(3))
+        far_arrive()
+        for s in (0, 6):
+            cats[s] = joined(wides[t][s])
+        q = coarsen(1, 1) + middle_q + coarsen(5, 2)
+        third = folded(partial + sum(dot(joined(q[s]), wmats[FAR + s - 2]) for s in (0, 4, 5)))
         owner = me + lane // (lanes // 4) - 1
         third = jnp.where((owner >= 0) & (owner < lats), third, 0.0)
         top = vertical(third, t, LEVELS)
         third = jnp.where(lane % (lanes // 4) < lanes // 16, top, vertical(third, t, 3))
         third = joined(third)
-        second = vertical(jnp.concatenate(q[1:4], axis=1), t, 2)
         lifted = []
         for s in (-1, 0, 1):
             c = folded(dot(third, wmats[FAR_T + s]))
@@ -360,14 +376,14 @@
             own = jnp.where(lane < r * (lanes // 4), own, turned)
         wide = wides[t]
         wide[3] = own
-        arrived = exchange([(d, wide.at[pl.ds(3, 1)], wide.at[pl.ds(3 - d, 1)]) for d in REACH])
+        moves = [(d, wide.at[pl.ds(3, 1)], wide.at[pl.ds(3 - d, 1)]) for d in REACH]
+        near_arrive, far_arrive = exchange(moves[:4]), exchange(moves[4:])
         weigh_second(t)
         second_arrive = share(seconds[t], quarter, 1)
-        k_arrive = share(ks[t], half_rows, 2 - t)
         if t == 0:
             build_third()
-        arrived()
-        before, own, after = deep(t)
+        before, own, after = deep(t, near_arrive, far_arrive)
+        k_arrive = share(ks[t], half_rows, 2 - t)
         for r in range(quarter):
             coarse = own if r == 0 else pltpu.roll(own, lanes - r * (lanes // 4), 1)
             g_second[r + 1] = lift_second(t, r, coarse)
@@ -430,12 +446,8 @@
 
 def on_device(increment, filter_taps, band_roots, lats):
     lev, tile, lanes = increment.shape
-    padded = -(-lev // 16) * 16
-    taps = make_filters(filter_taps).reshape(-1)
+    padded, side = -(-lev // 16) * 16, -(-lev // 128) * 128
     x = jnp.pad(jnp.transpose(increment, (1, 0, 2)), ((0, 0), (0, padded - lev), (0, 0)))
-    roots = jnp.pad(band_roots, ((0, 0), (0, padded - lev), (0, padded - lev)))
-    roots = jnp.concatenate([roots, jnp.swapaxes(roots, 1, 2)])
-
     def slabs(count):
         return pltpu.VMEM((count, padded, lanes), F32)
 
@@ -449,8 +461,12 @@
     scratch += [
         pltpu.VMEM((FAR_T + 2, 2 * lanes, 2 * lanes), BF16),
         pltpu.VMEM((2 * (LEVELS + 1), 2 * padded, padded), BF16),
+        pltpu.SMEM((filter_taps.size,), F32),
+        pltpu.VMEM(band_roots.shape, F32),
+        pltpu.VMEM((side, side), F32),
         pltpu.SemaphoreType.DMA((copies,)),
         pltpu.SemaphoreType.DMA((copies,)),
+        pltpu.SemaphoreType.DMA,
         pltpu.SemaphoreType.DMA,
     ]
     y = pl.pallas_call(
@@ -459,14 +475,14 @@
         in_specs=[
             pl.BlockSpec(memory_space=pltpu.SMEM),
             pl.BlockSpec(memory_space=pl.ANY),
-            pl.BlockSpec(memory_space=pltpu.VMEM),
+            pl.BlockSpec(memory_space=pl.ANY),
         ],
         out_specs=pl.BlockSpec(memory_space=pltpu.VMEM),
         scratch_shapes=scratch,
         compiler_params=pltpu.CompilerParams(
             collective_id=0, has_side_effects=True, vmem_limit_bytes=48 << 20
         ),
-    )(taps, x, roots)
+    )(filter_taps.reshape(-1), x, band_roots)
     return jnp.transpose(y[:, :lev], (1, 0, 2))
 
 

time: 56.7 us -> 54.6 us (0.963)
  other arithmetic: 1.68 us -> 0 us
    div x1 -> x0, other arithmetic: 0.75 us -> none  [make_filters(): ROOT_TWO * coeffs[:, :, 0]]
    unnamed x5 -> x3, local copies, waits for them, and re-layouts: 3.35 us -> 2.64 us
    convert_element_type x1 -> x0, other arithmetic: 0.7 us -> none  [make_filters(): coeffs = filter_taps.astype(F32)]
    reshape x1, local copies, waits for them, and re-layouts: 0.09 us -> 0.78 us  [on_device(): filter_taps.reshape(-1)]
where the time goes in v3:
time: 54.6 us; the launch traced here: 54.4 us
  Pallas kernels  49.4 us (90%)
  local copies, waits for them, and re-layouts  4.93 us (9%)
    pallas_call x1, Pallas kernels, on_device(): pl.pallas_call(functools.partial(kernel, lats), out_shape=jax.ShapeDtypeS...  49.4 us
    unnamed x3, local copies, waits for them, and re-layouts  2.64 us
    transpose x2, local copies, waits for them, and re-layouts, on_device(): return jnp.transpose(y[:, :lev], (1, 0, 2))  1.42 us

profile of v3, /device:TPU:3, one launch (start us, length us, event | category | flops | bytes accessed | tf_op | source)
XLA Modules:
  0.0 54.4 jit_solution(11398291507002908261)
XLA Ops:
  0.0 0.8 %reshape.3.raw_taps = s32[80]{0:T(128)S(1)} reshape(s32[4,2,2,5]{3,2,1,0:T(2,128)} %param.4) | data formatting | bytes 640 | tf_op jit(solution)/shard_map/reshape | solution.py:485
  0.8 1.6 %copy.7 = f32[137,16,128]{2,0,1:T(8,128)S(1)} copy(f32[137,16,128]{2,1,0:T(8,128)} %param.3) | data formatting | bytes 2244608 | tf_op args[0]
  2.4 0.0 copy-start
  2.4 0.1 pad.4.x_hbm
  2.5 1.0 %copy-done = f32[5,137,137]{2,1,0:T(8,128)S(1)} copy-done((f32[5,137,137]{2,1,0:T(8,128)S(1)}, f32[5,137,137]{2,1,0:T(8,128)}, u32[]{:S(2)}) %copy-start) | copy-done | bytes 375404
  3.5 49.4 %shard_map.37 = f32[16,144,128]{2,1,0:T(8,128)S(1)} custom-call(s32[80]{0:T(128)S(1)} %reshape.3.raw_taps, f32[16,144,128]{2,1,0:T(8,128)S(1)} %pad.4.x_hbm, f32[5,137,137]{2,1,0:T(8,128)S(1)} %copy-done), custom_call_target="tpu_custom_call" | custom-call | tf_op jit(solution)/shard_map/pallas_call | solution.py:472
  53.0 0.1 slice_bitcast_fusion
  53.1 1.3 %copy.5 = f32[137,16,128]{2,1,0:T(8,128)} copy(f32[137,16,128]{2,0,1:T(8,128)S(1)} %slice_bitcast_fusion) | data formatting | bytes 2244608 | tf_op jit(solution)/shard_map/transpose | solution.py:486
Async XLA Ops:
  2.4 1.1 %copy-start = (f32[5,137,137]{2,1,0:T(8,128)S(1)}, f32[5,137,137]{2,1,0:T(8,128)}, u32[]{:S(2)}) copy-start(f32[5,137,137]{2,1,0:T(8,128)} %roots_hbm.1) | copy-start | bytes 1126144

commit v4 on v3

--- a/solution.py
+++ b/solution.py
@@ -188,13 +188,16 @@
     fetch.wait()
     square[...] = jnp.zeros(square.shape, F32)
     count = roots.shape[1]
-    for b in range(LEVELS + 1):
-        square[pl.ds(0, count), pl.ds(0, count)] = roots[b]
-        whole = square[...]
-        for t, m in enumerate((whole, whole.T)):
+
+    def split_roots(t):
+        for b in range(LEVELS + 1):
+            square[pl.ds(0, count), pl.ds(0, count)] = roots[b]
+            m = square[...].T if t else square[...]
             high, low = halves_of(m[:lev, :lev])
             mats[t * (LEVELS + 1) + b, pl.ds(0, lev)] = high
             mats[t * (LEVELS + 1) + b, pl.ds(lev, lev)] = low
+
+    split_roots(0)
 
     def along_lon(x, at):
         high, low = halves_of(x)
@@ -207,7 +210,7 @@
         r = dot(mats[b], high)
         return r[:lev] + r[lev:] + dot(mats[b, pl.ds(0, lev)], low)
 
-    def loop(start, stop, body, step=2):
+    def loop(start, stop, body, step=3):
         count = max(stop - start, 0)
         whole = count // step
         if whole > 1:
@@ -365,7 +368,7 @@
         arrived = share_coarse(t)
         if t == 0:
             build_second()
-        loop(0, half_rows, lambda i: weigh_first(t, i))
+        loop(0, half_rows, lambda i: weigh_first(t, i), 4)
         loop(1, quarter - 1, lambda i: analyse(t, i))
         arrived()
         analyse(t, 0)
@@ -382,6 +385,7 @@
         second_arrive = share(seconds[t], quarter, 1)
         if t == 0:
             build_third()
+            split_roots(1)
         before, own, after = deep(t, near_arrive, far_arrive)
         k_arrive = share(ks[t], half_rows, 2 - t)
         for r in range(quarter):

time: 54.6 us -> 54.2 us (level)
  no operation moved by 1% of the time
where the time goes in v4:
time: 54.2 us; the launch traced here: 53.9 us
  Pallas kernels  49 us (90%)
  local copies, waits for them, and re-layouts  4.93 us (9%)
    pallas_call x1, Pallas kernels, on_device(): pl.pallas_call(functools.partial(kernel, lats), out_shape=jax.ShapeDtypeS...  49 us
    unnamed x3, local copies, waits for them, and re-layouts  2.64 us
    transpose x2, local copies, waits for them, and re-layouts, on_device(): return jnp.transpose(y[:, :lev], (1, 0, 2))  1.42 us

profile of v4, /device:TPU:3, one launch (start us, length us, event | category | flops | bytes accessed | tf_op | source)
XLA Modules:
  0.0 53.9 jit_solution(12523739424778425507)
XLA Ops:
  0.0 0.8 %reshape.3.raw_taps = s32[80]{0:T(128)S(1)} reshape(s32[4,2,2,5]{3,2,1,0:T(2,128)} %param.4) | data formatting | bytes 640 | tf_op jit(solution)/shard_map/reshape | solution.py:489
  0.8 1.6 %copy.7 = f32[137,16,128]{2,0,1:T(8,128)S(1)} copy(f32[137,16,128]{2,1,0:T(8,128)} %param.3) | data formatting | bytes 2244608 | tf_op args[0]
  2.4 0.0 copy-start
  2.4 0.1 pad.4.x_hbm
  2.5 1.0 %copy-done = f32[5,137,137]{2,1,0:T(8,128)S(1)} copy-done((f32[5,137,137]{2,1,0:T(8,128)S(1)}, f32[5,137,137]{2,1,0:T(8,128)}, u32[]{:S(2)}) %copy-start) | copy-done | bytes 375404
  3.5 49.0 %shard_map.37 = f32[16,144,128]{2,1,0:T(8,128)S(1)} custom-call(s32[80]{0:T(128)S(1)} %reshape.3.raw_taps, f32[16,144,128]{2,1,0:T(8,128)S(1)} %pad.4.x_hbm, f32[5,137,137]{2,1,0:T(8,128)S(1)} %copy-done), custom_call_target="tpu_custom_call" | custom-call | tf_op jit(solution)/shard_map/pallas_call | solution.py:476
  52.5 0.1 slice_bitcast_fusion
  52.6 1.3 %copy.5 = f32[137,16,128]{2,1,0:T(8,128)} copy(f32[137,16,128]{2,0,1:T(8,128)S(1)} %slice_bitcast_fusion) | data formatting | bytes 2244608 | tf_op jit(solution)/shard_map/transpose | solution.py:490
Async XLA Ops:
  2.4 1.1 %copy-start = (f32[5,137,137]{2,1,0:T(8,128)S(1)}, f32[5,137,137]{2,1,0:T(8,128)}, u32[]{:S(2)}) copy-start(f32[5,137,137]{2,1,0:T(8,128)} %roots_hbm.1) | copy-start | bytes 1126144
